TPU v7x, 256 devices: a whole 4x4x8 slice. The times are simulated.
256 devices in a mesh: dp: 64 (over z, y, core), section: 4 (over x).
Axes of the slice: x: 4, y: 4, z: 8, core: 2. Of those that a mesh axis runs over, the one named last changes fastest.
Arguments:
- hidden_in: bfloat16 [4, 2, 64, 4096], P('section', None, 'dp'), may hold values from -48 to 48
- grad_out: bfloat16 [2, 64, 4096], P(None, 'dp'), may hold values from -6 to 6
- weight_gate: bfloat16 [4, 14336, 4096], P('section', 'dp'), may hold values from -0.09375 to 0.09375
- weight_up: bfloat16 [4, 14336, 4096], P('section', 'dp'), may hold values from -0.09375 to 0.09375
- weight_down: bfloat16 [4, 14336, 4096], P('section', 'dp'), may hold values from -0.046875 to 0.046875
- gain: float32 [4, 4096], P('section'), may hold values from 0.5 to 1.5
- counts: int32 [2], replicated, may hold values from 1 to 64, 85 in all
Outputs:
- grad_inputs: bfloat16 [4, 2, 64, 4096], P('section', None, 'dp')
- gate_grads: bfloat16 [4, 14336, 4096], P('section', 'dp')
- up_grads: bfloat16 [4, 14336, 4096], P('section', 'dp')
- down_grads: bfloat16 [4, 14336, 4096], P('section', 'dp')
- gain_grads: float32 [4, 4096], P('section')
Inputs may be any that keep to these rules, and one draw needn't show every extreme that they name: The 2 counts sum to 85.
All inputs are finite; a program needn't handle non-finite values.
Results may differ from a plain program's by a relative error of at most 0.012.
Values may be sent and summed in bfloat16 or wider, within the bound.
No kernel may reach another device: no remote copies, remote signals or barrier semaphores. Data moves between devices by JAX's collectives and lax.ppermute only.
A program may use at most 128 MiB of HBM per device.

v0:
```python
import jax
import jax.numpy as jnp
from jax import lax
from jax.sharding import PartitionSpec as P


def from_behind(x, axis, by):
    size = lax.axis_size(axis)
    pairs = [(i, i + by) for i in range(size) if 0 <= i + by < size]
    return lax.ppermute(x, axis, pairs)


def norm_rows(layer_rows, gain_row):
    row_values = layer_rows.astype(jnp.float32)
    inv_rms = lax.rsqrt(jnp.mean(row_values * row_values, axis=-1, keepdims=True) + 1e-05)
    normed_rows = (row_values * inv_rms * gain_row).astype(jnp.bfloat16)
    return (inv_rms, normed_rows)


def unit_grads(upstream, gate_pre, up_pre, down_mat):
    sigmoid_pre = jax.nn.sigmoid(gate_pre)
    silu_pre = gate_pre * sigmoid_pre
    activation = (silu_pre * up_pre).astype(jnp.bfloat16)
    grad_act = lax.dot_general(
        upstream, down_mat, (((1,), (1,)), ((), ())), preferred_element_type=jnp.float32
    )
    grad_gate = (grad_act * up_pre * sigmoid_pre * (1.0 + gate_pre * (1.0 - sigmoid_pre))).astype(
        jnp.bfloat16
    )
    grad_up = (grad_act * silu_pre).astype(jnp.bfloat16)
    return (activation, grad_gate, grad_up)


def norm_back(layer_rows, inv_rms, upstream, grad_normed, gain_row):
    row_values = layer_rows.astype(jnp.float32)
    gained_grad = gain_row * grad_normed
    inner_sum = jnp.sum(gained_grad * row_values, axis=-1, keepdims=True)
    feature_count = row_values.shape[-1]
    grad_rows = (
        upstream.astype(jnp.float32)
        + inv_rms * gained_grad
        - row_values * inv_rms**3 * inner_sum / feature_count
    )
    return grad_rows.astype(jnp.bfloat16)


def transposed_product(left_rows, right_rows):
    return lax.dot_general(
        left_rows, right_rows, (((0,), (0,)), ((), ())), preferred_element_type=jnp.float32
    )


def pick_block(stacked, index_value):
    return lax.dynamic_index_in_dim(stacked, index_value, 0, keepdims=False)


def on_device(hidden_in, grad_out, weight_gate, weight_up, weight_down, gain, counts):
    section_count = lax.axis_size("section")
    section_pos = lax.axis_index("section")
    dp_pos = lax.axis_index("dp")
    layer_rows = hidden_in[0]
    gate_mat = weight_gate[0]
    up_mat = weight_up[0]
    down_mat = weight_down[0]
    gain_row = gain[0]
    batch_count, slot_local, feature_count = layer_rows.shape
    unit_count = gate_mat.shape[0]
    full_slots = slot_local * lax.axis_size("dp")
    slot_ids = dp_pos * slot_local + jnp.arange(slot_local)
    live_slots = slot_ids[None, :] < counts[:, None]
    top_local = jnp.where(live_slots[:, :, None], grad_out, jnp.zeros((), jnp.bfloat16))
    is_last = section_pos == section_count - 1
    top_whole = lax.all_gather(top_local, "dp", axis=1, tiled=True)
    received = jnp.zeros((full_slots, feature_count), jnp.bfloat16)
    gathered_all = lax.all_gather(layer_rows, "dp", axis=1, tiled=True)
    all_inv, all_normed = norm_rows(gathered_all, gain_row)
    all_gate = jnp.einsum("mpd,fd->mpf", all_normed, gate_mat, preferred_element_type=jnp.float32)
    all_up = jnp.einsum("mpd,fd->mpf", all_normed, up_mat, preferred_element_type=jnp.float32)
    grad_store = jnp.zeros_like(layer_rows)
    gate_total = jnp.zeros((unit_count, feature_count), jnp.float32)
    up_total = jnp.zeros((unit_count, feature_count), jnp.float32)
    down_total = jnp.zeros((unit_count, feature_count), jnp.float32)
    gain_total = jnp.zeros((feature_count,), jnp.float32)
    last_step = batch_count + section_count - 2
    for step_index in range(batch_count + section_count - 1):
        micro_index = step_index - (section_count - 1 - section_pos)
        is_valid = (micro_index >= 0) & (micro_index < batch_count)
        clamped = jnp.clip(micro_index, 0, batch_count - 1)
        gathered = pick_block(gathered_all, clamped)
        gate_pre = pick_block(all_gate, clamped)
        up_pre = pick_block(all_up, clamped)
        full_inv = pick_block(all_inv, clamped)
        full_normed = pick_block(all_normed, clamped)
        full_up = jnp.where(is_last, pick_block(top_whole, clamped), received)
        full_up = jnp.where(is_valid, full_up, jnp.zeros((), jnp.bfloat16))
        activation, grad_gate, grad_up = unit_grads(full_up, gate_pre, up_pre, down_mat)
        gate_total = gate_total + transposed_product(grad_gate, full_normed)
        up_total = up_total + transposed_product(grad_up, full_normed)
        down_total = down_total + transposed_product(activation, full_up)
        partial_sum = jnp.dot(grad_gate, gate_mat, preferred_element_type=jnp.float32) + jnp.dot(
            grad_up, up_mat, preferred_element_type=jnp.float32
        )
        grad_normed = lax.psum(partial_sum, "dp")
        grad_full = norm_back(gathered, full_inv, full_up, grad_normed, gain_row)
        gain_total = gain_total + jnp.sum(
            grad_normed * gathered.astype(jnp.float32) * full_inv, axis=0
        )
        grad_own = lax.dynamic_slice_in_dim(grad_full, dp_pos * slot_local, slot_local, 0)
        old_rows = pick_block(grad_store, clamped)
        grad_store = lax.dynamic_update_index_in_dim(
            grad_store, jnp.where(is_valid, grad_own, old_rows), clamped, 0
        )
        if step_index < last_step:
            received = from_behind(grad_full, "section", -1)
    return (
        grad_store[None],
        gate_total.astype(jnp.bfloat16)[None],
        up_total.astype(jnp.bfloat16)[None],
        down_total.astype(jnp.bfloat16)[None],
        gain_total[None],
    )


def solution(mesh):
    return jax.shard_map(
        on_device,
        mesh=mesh,
        in_specs=(
            P("section", None, "dp", None),
            P(None, "dp", None),
            P("section", "dp", None),
            P("section", "dp", None),
            P("section", "dp", None),
            P("section", None),
            P(),
        ),
        out_specs=(
            P("section", None, "dp", None),
            P("section", "dp", None),
            P("section", "dp", None),
            P("section", "dp", None),
            P("section", None),
        ),
        check_vma=False,
    )
```

profile of v0, /device:TPU:2, one launch (start us, length us, event | category | flops | bytes accessed | tf_op | source)
XLA Modules:
  0.0 1220.3 jit_solution(14955202066246153748)
XLA Ops:
  10.1 80.4 %all-gather.6.cloned.1.call-done = bf16[1,2,64,4096]{3,1,0,2:T(2,128)(2,1)} async-done(((bf16[1,2,1,4096]{3,1,0,2:T(2,128)(2,1)}), bf16[1,2,64,4096]{3,1,0,2:T(2,128)(2,1)}) %all-gather.6.cloned.1.call-update) | async-done | bytes 1048592 | tf_op jit(solution)/shard_map/all_gather | solution.py:75
  97.3 71.2 %all-gather.4.cloned.1.call-done = bf16[2,64,4096]{2,0,1:T(2,128)(2,1)} async-done(((bf16[2,1,4096]{2,0,1:T(2,128)(2,1)}), bf16[2,64,4096]{2,0,1:T(2,128)(2,1)}) %all-gather.4.cloned.1.call-update) | async-done | bytes 1048592 | tf_op jit(solution)/shard_map/all_gather | solution.py:73
  168.5 9.9 constant_dynamic-slice_fusion.1
  187.0 2.9 fusion.147
  189.8 177.9 %all-reduce.6.cloned.1.call-done = f32[64,4096]{1,0:T(8,128)} async-done(((f32[64,4096]{1,0:T(8,128)}), f32[64,4096]{1,0:T(8,128)}) %all-reduce.6.cloned.1.call-update) | async-done | bytes 1048592 | tf_op jit(solution)/shard_map/psum | solution.py:103
  370.1 2.6 fusion.43
  372.7 2.6 collective-permute-start
  375.4 2.6 fusion.88
  380.2 5.8 collective-permute-done
  393.9 4.5 convolution_add_fusion.5
  398.4 177.5 %all-reduce.8.cloned.1.call-done = f32[64,4096]{1,0:T(8,128)} async-done(((f32[64,4096]{1,0:T(8,128)}), f32[64,4096]{1,0:T(8,128)}) %all-reduce.8.cloned.1.call-update) | async-done | bytes 1048592 | tf_op jit(solution)/shard_map/psum | solution.py:103
  579.8 2.6 collective-permute-start.1
  582.5 4.8 convolution_add_fusion.9
  587.3 2.5 convolution_add_fusion.1
  589.8 3.5 collective-permute-done.1
  600.6 4.5 convolution_add_fusion.4
  605.1 178.0 %all-reduce.10.cloned.1.call-done = f32[64,4096]{1,0:T(8,128)} async-done(((f32[64,4096]{1,0:T(8,128)}), f32[64,4096]{1,0:T(8,128)}) %all-reduce.10.cloned.1.call-update) | async-done | bytes 1048592 | tf_op jit(solution)/shard_map/psum | solution.py:103
  787.8 2.6 collective-permute-start.2
  790.4 4.6 convolution_add_fusion.8
  798.0 3.5 collective-permute-done.2
  809.1 4.7 convolution_add_fusion.3
  813.8 2.6 convolution_add_fusion.7
  816.3 178.0 %all-reduce.12.cloned.1.call-done = f32[64,4096]{1,0:T(8,128)} async-done(((f32[64,4096]{1,0:T(8,128)}), f32[64,4096]{1,0:T(8,128)}) %all-reduce.12.cloned.1.call-update) | async-done | bytes 1048592 | tf_op jit(solution)/shard_map/psum | solution.py:103
  999.1 2.6 collective-permute-start.3
  1001.7 2.5 fusion.143
  1006.4 6.3 collective-permute-done.3
  1016.4 2.6 fusion.145
  1022.0 4.1 fusion.6
  1026.1 2.8 fusion.7
  1029.0 4.1 fusion.5
  1033.1 174.6 %all-reduce.14.cloned.1.call-done = f32[64,4096]{1,0:T(8,128)} async-done(((f32[64,4096]{1,0:T(8,128)}), f32[64,4096]{1,0:T(8,128)}) %all-reduce.14.cloned.1.call-update) | async-done | bytes 1048592 | tf_op jit(solution)/shard_map/psum | solution.py:103
  1209.8 2.8 fusion.153
  (184 shorter events, 73.6 us)
Async XLA Ops:
  7.2 87.8 %copy-start = (bf16[1,224,4096]{2,1,0:T(8,128)(2,1)S(1)}, bf16[1,224,4096]{2,1,0:T(8,128)(2,1)}, u32[]{:S(2)}) copy-start(bf16[1,224,4096]{2,1,0:T(8,128)(2,1)} %param.9) | copy-start | bytes 5505028
  7.2 83.4 %all-gather.6.cloned.1.call-start = ((), (), s32[]{:S(2)}) async-start(), calls=%async_computation.6 | async-start | bytes 1064960 | tf_op jit(solution)/shard_map/all_gather | solution.py:75
  7.9 160.6 %all-gather.4.cloned.1.call-start = ((), (), s32[]{:S(2)}) async-start(), calls=%async_computation | async-start | bytes 1064960 | tf_op jit(solution)/shard_map/all_gather | solution.py:73
  10.1 357.7 %all-reduce.6.cloned.1.call-start = ((), (), s32[]{:S(2)}) async-start(), calls=%async_computation.1 | async-start | bytes 2097152 | tf_op jit(solution)/shard_map/psum | solution.py:103
  97.3 89.6 %copy-start.29 = (f32[2,64,224]{2,1,0:T(8,128)}, f32[2,64,224]{2,1,0:T(8,128)S(1)}, u32[]{:S(2)}) copy-start(f32[2,64,224]{2,1,0:T(8,128)S(1)} %fusion.23) | copy-start | bytes 344068
  168.5 10.0 copy-start.12
  182.3 393.6 %all-reduce.8.cloned.1.call-start = ((), (), s32[]{:S(2)}) async-start(), calls=%async_computation.2 | async-start | bytes 2097152 | tf_op jit(solution)/shard_map/psum | solution.py:103
  187.0 191.0 %copy-start.58 = (f32[64]{0:T(128)}, f32[64]{0:T(128)S(1)}, u32[]{:S(2)}) copy-start(f32[64]{0:T(128)S(1)} %get-tuple-element.16) | copy-start | bytes 772
  187.0 180.8 %copy-start.35 = (f32[1,4096]{1,0:T(1,128)S(1)}, f32[1,4096]{1,0:T(1,128)}, u32[]{:S(2)}) copy-start(f32[1,4096]{1,0:T(1,128)} %param.12) | copy-start | bytes 49156
  372.7 13.2 %collective-permute-start = (bf16[64,4096]{1,0:T(8,128)(2,1)S(1)}, bf16[64,4096]{1,0:T(8,128)(2,1)S(1)}, u32[]{:S(2)}, u32[]{:S(2)}) collective-permute-start(bf16[64,4096]{1,0:T(8,128)(2,1)S(1)} %fusion.43), channel_id=1, source_target_pairs={{1,0},{2,1},{3,2},{5,4},{6,5},{7,6},{9,8},{10,9},{11,10},{13,12},{... | collective-permute-start | bytes 1572872 | tf_op jit(solution)/shard_map/ppermute | solution.py:10
  377.9 8.0 copy-start.28
  379.1 7.5 copy-start.13
  379.1 7.5 copy-start.30
  390.4 392.7 %all-reduce.10.cloned.1.call-start = ((), (), s32[]{:S(2)}) async-start(), calls=%async_computation.3 | async-start | bytes 2097152 | tf_op jit(solution)/shard_map/psum | solution.py:103
  579.8 7.4 copy-start.37
  579.8 7.4 copy-start.31
  579.8 13.4 %collective-permute-start.1 = (bf16[64,4096]{1,0:T(8,128)(2,1)S(1)}, bf16[64,4096]{1,0:T(8,128)(2,1)S(1)}, u32[]{:S(2)}, u32[]{:S(2)}) collective-permute-start(bf16[64,4096]{1,0:T(8,128)(2,1)S(1)} %fusion.50), channel_id=1, source_target_pairs={{1,0},{2,1},{3,2},{5,4},{6,5},{7,6},{9,8},{10,9},{11,10},{13,12},{... | collective-permute-start | bytes 1572872 | tf_op jit(solution)/shard_map/ppermute | solution.py:10
  593.9 191.6 %copy-start.23 = (bf16[64,4096]{1,0:T(8,128)(2,1)}, bf16[64,4096]{1,0:T(8,128)(2,1)S(1)}, u32[]{:S(2)}) copy-start(bf16[64,4096]{1,0:T(8,128)(2,1)S(1)} %fusion.73) | copy-start | bytes 1572868
  597.6 396.7 %all-reduce.12.cloned.1.call-start = ((), (), s32[]{:S(2)}) async-start(), calls=%async_computation.4 | async-start | bytes 2097152 | tf_op jit(solution)/shard_map/psum | solution.py:103
  783.1 7.3 copy-start.46
  787.8 7.2 copy-start.39
  787.8 13.6 %collective-permute-start.2 = (bf16[64,4096]{1,0:T(8,128)(2,1)}, bf16[64,4096]{1,0:T(8,128)(2,1)S(1)}, u32[]{:S(2)}, u32[]{:S(2)}) collective-permute-start(bf16[64,4096]{1,0:T(8,128)(2,1)} %fusion.57), channel_id=1, source_target_pairs={{1,0},{2,1},{3,2},{5,4},{6,5},{7,6},{9,8},{10,9},{11,10},{13,12},{... | collective-permute-start | bytes 1572872 | tf_op jit(solution)/shard_map/ppermute | solution.py:10
  808.8 398.8 %all-reduce.14.cloned.1.call-start = ((), (), s32[]{:S(2)}) async-start(), calls=%async_computation.5 | async-start | bytes 2097152 | tf_op jit(solution)/shard_map/psum | solution.py:103
  994.3 7.3 copy-start.32
  999.1 13.7 %collective-permute-start.3 = (bf16[64,4096]{1,0:T(8,128)(2,1)}, bf16[64,4096]{1,0:T(8,128)(2,1)}, u32[]{:S(2)}, u32[]{:S(2)}) collective-permute-start(bf16[64,4096]{1,0:T(8,128)(2,1)} %fusion.64), channel_id=1, source_target_pairs={{1,0},{2,1},{3,2},{5,4},{6,5},{7,6},{9,8},{10,9},{11,10},{13,12},{... | collective-permute-start | bytes 1572872 | tf_op jit(solution)/shard_map/ppermute | solution.py:10
  1006.4 8.4 copy-start.16
  1029.0 178.7 %copy-start.11 = (bf16[1,2,64,4096]{3,2,1,0:T(8,128)(2,1)S(1)}, bf16[1,2,64,4096]{3,2,1,0:T(8,128)(2,1)}, u32[]{:S(2)}) copy-start(bf16[1,2,64,4096]{3,2,1,0:T(8,128)(2,1)} %copy.28) | copy-start | bytes 3145732
  1033.0 176.8 %copy-start.41 = (bf16[2,1,4096]{2,0,1:T(2,128)(2,1)S(1)}, bf16[2,1,4096]{2,0,1:T(2,128)(2,1)}, u32[]{:S(2)}) copy-start(bf16[2,1,4096]{2,0,1:T(2,128)(2,1)} %dynamic_update_slice.20) | copy-start | bytes 49156
  1033.0 179.8 %copy-start.54 = (f32[4096]{0:T(1024)S(1)}, f32[4096]{0:T(1024)}, u32[]{:S(2)}) copy-start(f32[4096]{0:T(1024)} %get-tuple-element.7) | copy-start | bytes 49156
  1033.0 179.8 %copy-start.55 = (f32[4096]{0:T(1024)S(1)}, f32[4096]{0:T(1024)}, u32[]{:S(2)}) copy-start(f32[4096]{0:T(1024)} %get-tuple-element.5) | copy-start | bytes 49156
  1033.0 179.8 %copy-start.56 = (f32[4096]{0:T(1024)S(1)}, f32[4096]{0:T(1024)}, u32[]{:S(2)}) copy-start(f32[4096]{0:T(1024)} %get-tuple-element.9) | copy-start | bytes 49156
  1033.0 179.8 %copy-start.57 = (f32[4096]{0:T(1024)S(1)}, f32[4096]{0:T(1024)}, u32[]{:S(2)}) copy-start(f32[4096]{0:T(1024)} %get-tuple-element.11) | copy-start | bytes 49156
  (38 other events, 107.2 us)
Sparse Core Ops, SparseCore 0:
  10.8 79.7 all-gather.5
  93.9 74.5 all-gather.3
  182.4 185.2 all-reduce.5
  390.5 185.3 all-reduce.7
  597.7 185.3 all-reduce.9
  808.9 185.3 all-reduce.11
  1022.1 185.4 all-reduce.13
where the time goes:
time: 1220 us
  waiting for transfers between devices  1060 us (87%)
  matrix products  68.6 us (6%)
  other arithmetic  42.1 us (3%)
  local copies, waits for them, and re-layouts  26.6 us (2%)
  between operations  14.8 us (1%)
    psum x5, waiting for transfers between devices, on_device(): grad_normed = lax.psum(partial_sum, 'dp')  886 us
    all_gather x1, waiting for transfers between devices, on_device(): gathered_all = lax.all_gather(layer_rows, 'dp', axis=1, tiled=True)  80.4 us
    all_gather x1, waiting for transfers between devices, on_device(): top_whole = lax.all_gather(top_local, 'dp', axis=1, tiled=True)  71.2 us
    dot_general x15, matrix products, transposed_product(): lax.dot_general(left_rows, right_rows, (((0,), (0,)), ((), ())), preferre...  52.1 us
  transfers between devices with their start and end apart: 11, of which 11 were waited for; matrix products, arithmetic and copies ran while one was open for 6% of the time, Pallas kernels for 0%

commit v1 on v0

--- a/solution.py
+++ b/solution.py
@@ -100,7 +100,13 @@
         partial_sum = jnp.dot(grad_gate, gate_mat, preferred_element_type=jnp.float32) + jnp.dot(
             grad_up, up_mat, preferred_element_type=jnp.float32
         )
-        grad_normed = lax.psum(partial_sum, "dp")
+
+        def watch_the_roads(my_tile):
+            a_now = jax.lax.all_gather(my_tile, axis_name="dp")
+            b_now = jnp.sum(a_now, axis=0)
+            return b_now
+
+        grad_normed = watch_the_roads(partial_sum)
         grad_full = norm_back(gathered, full_inv, full_up, grad_normed, gain_row)
         gain_total = gain_total + jnp.sum(
             grad_normed * gathered.astype(jnp.float32) * full_inv, axis=0

time: 1220 us -> 1580 us (1.30)
  waiting for transfers between devices: 1060 us -> 1310 us
  other arithmetic: 42.1 us -> 154 us
    all_gather x0 -> x5, waiting for transfers between devices: none -> 1100 us  [watch_the_roads(): a_now = jax.lax.all_gather(my_tile, axis_name='dp')]
    psum x5 -> x0, waiting for transfers between devices: 886 us -> none  [on_device(): grad_normed = lax.psum(partial_sum, 'dp')]
    reduce_sum x0 -> x5, other arithmetic: none -> 108 us  [watch_the_roads(): b_now = jnp.sum(a_now, axis=0)]
    ppermute x4, waiting for transfers between devices: 19 us -> 54.5 us  [from_behind(): return lax.ppermute(x, axis, pairs)]
  transfers between devices with their start and end apart: 11 -> 11, of which waited for: 11 -> 11; matrix products, arithmetic and copies ran while one was open for 6% -> 4% of each run, Pallas kernels for 0% -> 0%
where the time goes in v1:
time: 1580 us
  waiting for transfers between devices  1310 us (83%)
  other arithmetic  154 us (10%)
  matrix products  58.3 us (4%)
  local copies, waits for them, and re-layouts  30.5 us (2%)
    all_gather x5, waiting for transfers between devices, watch_the_roads(): a_now = jax.lax.all_gather(my_tile, axis_name='dp')  1100 us
    reduce_sum x5, other arithmetic, watch_the_roads(): b_now = jnp.sum(a_now, axis=0)  108 us
    all_gather x1, waiting for transfers between devices, on_device(): gathered_all = lax.all_gather(layer_rows, 'dp', axis=1, tiled=True)  80.4 us
    all_gather x1, waiting for transfers between devices, on_device(): top_whole = lax.all_gather(top_local, 'dp', axis=1, tiled=True)  71.7 us
    ppermute x4, waiting for transfers between devices, from_behind(): return lax.ppermute(x, axis, pairs)  54.5 us
    dot_general x15, matrix products, transposed_product(): lax.dot_general(left_rows, right_rows, (((0,), (0,)), ((), ())), preferre...  42.7 us
  transfers between devices with their start and end apart: 11, of which 11 were waited for; matrix products, arithmetic and copies ran while one was open for 4% of the time, Pallas kernels for 0%

profile of v1, /device:TPU:2, one launch (start us, length us, event | category | flops | bytes accessed | tf_op | source)
XLA Modules:
  0.0 1577.9 jit_solution(7232983707224274253)
XLA Ops:
  10.1 80.4 %all-gather.16.cloned.1.call-done = bf16[1,2,64,4096]{3,1,0,2:T(2,128)(2,1)} async-done(((bf16[1,2,1,4096]{3,1,0,2:T(2,128)(2,1)}), bf16[1,2,64,4096]{3,1,0,2:T(2,128)(2,1)}) %all-gather.16.cloned.1.call-update) | async-done | bytes 1048592 | tf_op jit(solution)/shard_map/all_gather | solution.py:75
  96.7 71.7 %all-gather.14.cloned.1.call-done = bf16[2,64,4096]{2,0,1:T(2,128)(2,1)} async-done(((bf16[2,1,4096]{2,0,1:T(2,128)(2,1)}), bf16[2,64,4096]{2,0,1:T(2,128)(2,1)}) %all-gather.14.cloned.1.call-update) | async-done | bytes 1048592 | tf_op jit(solution)/shard_map/all_gather | solution.py:73
  168.5 10.1 constant_dynamic-slice_fusion.1
  182.6 2.8 copy.33
  186.0 230.4 %all-gather.18.cloned.1.call-done = f32[4096,4096]{1,0:T(8,128)} async-done(((f32[64,4096]{1,0:T(8,128)}), f32[4096,4096]{1,0:T(8,128)}) %all-gather.18.cloned.1.call-update) | async-done | bytes 67108880 | tf_op jit(solution)/shard_map/all_gather | solution.py:105
  416.4 21.7 %reduce_sum.145 = f32[64,4096]{1,0:T(8,128)} reduce(f32[64,64,4096]{2,1,0:T(8,128)} %bitcast.13, f32[]{:T(128)} %constant.130.clone.1), dimensions={0}, to_apply=%region_1.2 | reduce | flops 16515072 | bytes 68157440 | tf_op jit(solution)/shard_map/reduce_sum | solution.py:106
  440.4 2.5 fusion.43
  442.9 2.6 collective-permute-start
  445.6 13.4 collective-permute-done
  465.6 233.1 %all-gather.20.cloned.1.call-done = f32[4096,4096]{1,0:T(8,128)} async-done(((f32[64,4096]{1,0:T(8,128)}), f32[4096,4096]{1,0:T(8,128)}) %all-gather.20.cloned.1.call-update) | async-done | bytes 67108880 | tf_op jit(solution)/shard_map/all_gather | solution.py:105
  698.7 21.7 %reduce_sum.147 = f32[64,4096]{1,0:T(8,128)} reduce(f32[64,64,4096]{2,1,0:T(8,128)} %bitcast.21, f32[]{:T(128)} %constant.130.clone.1), dimensions={0}, to_apply=%region_3.4 | reduce | flops 16515072 | bytes 68157440 | tf_op jit(solution)/shard_map/reduce_sum | solution.py:106
  727.5 13.8 collective-permute-done.1
  747.1 233.1 %all-gather.22.cloned.1.call-done = f32[4096,4096]{1,0:T(8,128)} async-done(((f32[64,4096]{1,0:T(8,128)}), f32[4096,4096]{1,0:T(8,128)}) %all-gather.22.cloned.1.call-update) | async-done | bytes 67108880 | tf_op jit(solution)/shard_map/all_gather | solution.py:105
  980.2 21.7 %reduce_sum.149 = f32[64,4096]{1,0:T(8,128)} reduce(f32[64,64,4096]{2,1,0:T(8,128)} %bitcast.30, f32[]{:T(128)} %constant.130.clone.1), dimensions={0}, to_apply=%region_5.6 | reduce | flops 16515072 | bytes 68157440 | tf_op jit(solution)/shard_map/reduce_sum | solution.py:106
  1009.0 13.8 collective-permute-done.2
  1028.6 233.1 %all-gather.24.cloned.1.call-done = f32[4096,4096]{1,0:T(8,128)} async-done(((f32[64,4096]{1,0:T(8,128)}), f32[4096,4096]{1,0:T(8,128)}) %all-gather.24.cloned.1.call-update) | async-done | bytes 67108880 | tf_op jit(solution)/shard_map/all_gather | solution.py:105
  1261.7 21.7 %reduce_sum.151 = f32[64,4096]{1,0:T(8,128)} reduce(f32[64,64,4096]{2,1,0:T(8,128)} %bitcast.39, f32[]{:T(128)} %constant.130.clone.1), dimensions={0}, to_apply=%region_7.8 | reduce | flops 16515072 | bytes 68157440 | tf_op jit(solution)/shard_map/reduce_sum | solution.py:106
  1288.1 2.7 collective-permute-start.3
  1290.8 13.6 collective-permute-done.3
  1312.7 3.2 fusion.88
  1318.4 2.9 fusion.147
  1325.8 4.7 convolution_add_fusion.9
  1330.6 2.5 convolution_add_fusion.5
  1333.9 2.5 convolution_add_fusion.1
  1338.7 4.7 convolution_add_fusion.8
  1343.5 2.6 convolution_add_fusion.4
  1349.0 3.4 fusion.143
  1355.6 2.6 convolution_add_fusion.3
  1359.8 4.1 fusion.7
  1370.2 173.1 %all-gather.26.cloned.1.call-done = f32[4096,4096]{1,0:T(8,128)} async-done(((f32[64,4096]{1,0:T(8,128)}), f32[4096,4096]{1,0:T(8,128)}) %all-gather.26.cloned.1.call-update) | async-done | bytes 67108880 | tf_op jit(solution)/shard_map/all_gather | solution.py:105
  1543.3 21.7 %reduce_sum.153 = f32[64,4096]{1,0:T(8,128)} reduce(f32[64,64,4096]{2,1,0:T(8,128)} %bitcast.49, f32[]{:T(128)} %constant.130.clone.1), dimensions={0}, to_apply=%region_9.10 | reduce | flops 16515072 | bytes 68157440 | tf_op jit(solution)/shard_map/reduce_sum | solution.py:106
  1567.3 3.0 fusion.153
  (215 shorter events, 88.3 us)
Async XLA Ops:
  7.2 88.0 %copy-start = (bf16[1,224,4096]{2,1,0:T(8,128)(2,1)S(1)}, bf16[1,224,4096]{2,1,0:T(8,128)(2,1)}, u32[]{:S(2)}) copy-start(bf16[1,224,4096]{2,1,0:T(8,128)(2,1)} %param.9) | copy-start | bytes 5505028
  7.2 83.4 %all-gather.16.cloned.1.call-start = ((), (), s32[]{:S(2)}) async-start(), calls=%async_computation.1 | async-start | bytes 1064960 | tf_op jit(solution)/shard_map/all_gather | solution.py:75
  7.9 160.6 %all-gather.14.cloned.1.call-start = ((), (), s32[]{:S(2)}) async-start(), calls=%async_computation | async-start | bytes 1064960 | tf_op jit(solution)/shard_map/all_gather | solution.py:73
  10.1 406.4 %all-gather.18.cloned.1.call-start = ((), (), s32[]{:S(2)}) async-start(), calls=%async_computation.2 | async-start | bytes 68157440 | tf_op jit(solution)/shard_map/all_gather | solution.py:105
  96.7 81.9 %copy-start.34 = (f32[2,64,224]{2,1,0:T(8,128)}, f32[2,64,224]{2,1,0:T(8,128)S(1)}, u32[]{:S(2)}) copy-start(f32[2,64,224]{2,1,0:T(8,128)S(1)} %fusion.23) | copy-start | bytes 344068
  168.5 10.1 copy-start.9
  182.6 516.2 %all-gather.20.cloned.1.call-start = ((), (), s32[]{:S(2)}) async-start(), calls=%async_computation.3 | async-start | bytes 68157440 | tf_op jit(solution)/shard_map/all_gather | solution.py:105
  186.0 252.1 %copy-start.70 = (f32[64]{0:T(128)}, f32[64]{0:T(128)S(1)}, u32[]{:S(2)}) copy-start(f32[64]{0:T(128)S(1)} %get-tuple-element.48) | copy-start | bytes 772
  416.4 21.7 %copy-start.41 = (f32[1,4096]{1,0:T(1,128)S(1)}, f32[1,4096]{1,0:T(1,128)}, u32[]{:S(2)}) copy-start(f32[1,4096]{1,0:T(1,128)} %param.12) | copy-start | bytes 49156
  442.9 16.1 %copy-start.42 = (bf16[64,4096]{1,0:T(8,128)(2,1)}, bf16[64,4096]{1,0:T(8,128)(2,1)S(1)}, u32[]{:S(2)}) copy-start(bf16[64,4096]{1,0:T(8,128)(2,1)S(1)} %fusion.43) | copy-start | bytes 1572868
  442.9 16.1 %collective-permute-start = (bf16[64,4096]{1,0:T(8,128)(2,1)S(1)}, bf16[64,4096]{1,0:T(8,128)(2,1)}, u32[]{:S(2)}, u32[]{:S(2)}) collective-permute-start(bf16[64,4096]{1,0:T(8,128)(2,1)S(1)} %fusion.43), channel_id=1, source_target_pairs={{1,0},{2,1},{3,2},{5,4},{6,5},{7,6},{9,8},{10,9},{11,10},{13,12},{... | collective-permute-start | bytes 1572872 | tf_op jit(solution)/shard_map/ppermute | solution.py:10
  445.6 15.4 copy-start.10
  465.6 514.6 %all-gather.22.cloned.1.call-start = ((), (), s32[]{:S(2)}) async-start(), calls=%async_computation.4 | async-start | bytes 68157440 | tf_op jit(solution)/shard_map/all_gather | solution.py:105
  725.0 16.3 %collective-permute-start.1 = (bf16[64,4096]{1,0:T(8,128)(2,1)}, bf16[64,4096]{1,0:T(8,128)(2,1)}, u32[]{:S(2)}, u32[]{:S(2)}) collective-permute-start(bf16[64,4096]{1,0:T(8,128)(2,1)} %fusion.50), channel_id=1, source_target_pairs={{1,0},{2,1},{3,2},{5,4},{6,5},{7,6},{9,8},{10,9},{11,10},{13,12},{... | collective-permute-start | bytes 1572872 | tf_op jit(solution)/shard_map/ppermute | solution.py:10
  727.5 15.8 %copy-start.11 = (bf16[1,224,4096]{2,1,0:T(8,128)(2,1)S(1)}, bf16[1,224,4096]{2,1,0:T(8,128)(2,1)}, u32[]{:S(2)}) copy-start(bf16[1,224,4096]{2,1,0:T(8,128)(2,1)} %param.11) | copy-start | bytes 5505028
  727.5 15.8 %copy-start.35 = (f32[2,64,224]{2,1,0:T(8,128)S(1)}, f32[2,64,224]{2,1,0:T(8,128)}, u32[]{:S(2)}) copy-start(f32[2,64,224]{2,1,0:T(8,128)} %copy-done.34) | copy-start | bytes 344068
  747.1 514.7 %all-gather.24.cloned.1.call-start = ((), (), s32[]{:S(2)}) async-start(), calls=%async_computation.5 | async-start | bytes 68157440 | tf_op jit(solution)/shard_map/all_gather | solution.py:105
  1006.6 16.3 %collective-permute-start.2 = (bf16[64,4096]{1,0:T(8,128)(2,1)}, bf16[64,4096]{1,0:T(8,128)(2,1)}, u32[]{:S(2)}, u32[]{:S(2)}) collective-permute-start(bf16[64,4096]{1,0:T(8,128)(2,1)} %fusion.57), channel_id=1, source_target_pairs={{1,0},{2,1},{3,2},{5,4},{6,5},{7,6},{9,8},{10,9},{11,10},{13,12},{... | collective-permute-start | bytes 1572872 | tf_op jit(solution)/shard_map/ppermute | solution.py:10
  1009.0 15.8 %copy-start.12 = (bf16[1,224,4096]{2,1,0:T(8,128)(2,1)S(1)}, bf16[1,224,4096]{2,1,0:T(8,128)(2,1)}, u32[]{:S(2)}) copy-start(bf16[1,224,4096]{2,1,0:T(8,128)(2,1)} %param.11) | copy-start | bytes 5505028
  1009.0 15.8 %copy-start.36 = (f32[2,64,224]{2,1,0:T(8,128)S(1)}, f32[2,64,224]{2,1,0:T(8,128)}, u32[]{:S(2)}) copy-start(f32[2,64,224]{2,1,0:T(8,128)} %copy-done.34) | copy-start | bytes 344068
  1028.6 514.7 %all-gather.26.cloned.1.call-start = ((), (), s32[]{:S(2)}) async-start(), calls=%async_computation.6 | async-start | bytes 68157440 | tf_op jit(solution)/shard_map/all_gather | solution.py:105
  1288.1 16.3 %collective-permute-start.3 = (bf16[64,4096]{1,0:T(8,128)(2,1)}, bf16[64,4096]{1,0:T(8,128)(2,1)}, u32[]{:S(2)}, u32[]{:S(2)}) collective-permute-start(bf16[64,4096]{1,0:T(8,128)(2,1)} %fusion.64), channel_id=1, source_target_pairs={{1,0},{2,1},{3,2},{5,4},{6,5},{7,6},{9,8},{10,9},{11,10},{13,12},{... | collective-permute-start | bytes 1572872 | tf_op jit(solution)/shard_map/ppermute | solution.py:10
  1290.8 15.6 copy-start.13
  1290.8 15.6 copy-start.37
  1338.7 4.7 copy-start.53
  1343.5 5.5 copy-start.27
  1543.3 21.7 %copy-start.8 = (bf16[1,2,64,4096]{3,2,1,0:T(8,128)(2,1)S(1)}, bf16[1,2,64,4096]{3,2,1,0:T(8,128)(2,1)}, u32[]{:S(2)}) copy-start(bf16[1,2,64,4096]{3,2,1,0:T(8,128)(2,1)} %copy.33) | copy-start | bytes 3145732
  1543.3 21.7 %copy-start.71 = (f32[64]{0:T(128)S(1)}, f32[64]{0:T(128)}, u32[]{:S(2)}) copy-start(f32[64]{0:T(128)} %get-tuple-element.16) | copy-start | bytes 772
  1565.0 5.4 copy-start.66
  1565.0 5.4 copy-start.67
  1565.0 5.4 copy-start.68
  1565.0 5.4 copy-start.69
  (51 other events, 116.3 us)
Sparse Core Ops, SparseCore 0:
  10.8 79.7 all-gather.15
  93.9 74.5 all-gather.13
  182.7 233.6 all-gather.17
  465.7 232.9 all-gather.19
  747.2 232.9 all-gather.21
  1028.7 232.9 all-gather.23
  1310.3 232.9 all-gather.25
